TPU v7x, 32 devices: a whole 2x2x4 slice. The times are simulated.
32 devices in a mesh: tok: 2 (over x), voc: 16 (over z, y, core).
Axes of the slice: x: 2, y: 2, z: 4, core: 2. Of those that a mesh axis runs over, the one named last changes fastest.
Arguments:
- hidden: bfloat16 [64, 4608], P(('tok', 'voc')), may hold values from -6 to 6
- norm_gain: float32 [4608], replicated, may hold values from 0.25 to 1.75
- head_weight: bfloat16 [16384, 4608], P(('tok', 'voc')), may hold values from -0.26367188 to 0.26367188
- targets: int32 [64], replicated, may hold values from 0 to 16383
- lengths: int32 [2], replicated, may hold values from 1 to 32
Outputs:
- token_loss: float32 [64], P(('tok', 'voc'))
- mean_loss: float32 [], replicated
All inputs are finite; a program needn't handle non-finite values.
Results may differ from a plain program's by a relative error of at most 0.00051.
Values may be sent and summed in bfloat16 or wider, within the bound.
A program may use at most 64 MiB of HBM per device.

v0:
```python
import jax
import jax.numpy as jnp
from jax import lax
from jax.sharding import PartitionSpec as P

WINDOW = 32


def body(hidden, norm_gain, head_weight, targets, lengths):
    own_rows = hidden.shape[0]
    vocab_rows = head_weight.shape[0]
    everyone = lax.axis_size(("tok", "voc"))
    whole = own_rows * everyone
    window = WINDOW
    me = lax.axis_index(("tok", "voc"))
    values = hidden.astype(jnp.float32)
    meansq = jnp.mean(values * values, axis=1, keepdims=True)
    normed = (values * lax.rsqrt(meansq + 1e-06) * norm_gain[None, :]).astype(jnp.bfloat16)
    offset = me * vocab_rows
    column = jnp.arange(vocab_rows, dtype=jnp.int32)
    grouped = lax.all_gather(normed, "voc", axis=0, tiled=True)
    logits = lax.dot_general(
        lax.all_gather(grouped, "tok", axis=0, tiled=True),
        head_weight,
        (((1,), (1,)), ((), ())),
        preferred_element_type=jnp.float32,
    )
    capped = 30.0 * jnp.tanh(logits / 30.0)
    expsum = jnp.sum(jnp.exp(capped), axis=1)
    wanted = targets - offset
    match = column[None, :] == wanted[:, None]
    picked = jnp.sum(jnp.where(match, capped, jnp.zeros_like(capped)), axis=1)
    stats = jnp.stack([expsum, picked])
    position = jnp.arange(window, dtype=jnp.int32)
    live_all = (position[None, :] < lengths[:, None]).astype(jnp.float32).reshape(whole)
    count = jnp.sum(lengths.astype(jnp.float32))
    totals = lax.psum(stats, ("tok", "voc"))
    loss_all = live_all * (jnp.log(totals[0]) - totals[1])
    mean_loss = jnp.sum(loss_all) / count
    token_loss = lax.dynamic_slice_in_dim(loss_all, me * own_rows, own_rows, 0)
    return (token_loss, mean_loss)


def solution(mesh):
    in_specs = (P(("tok", "voc"), None), P(), P(("tok", "voc"), None), P(), P())
    out_specs = (P(("tok", "voc")), P())
    return jax.shard_map(body, mesh=mesh, in_specs=in_specs, out_specs=out_specs, check_vma=False)
```

profile of v0, /device:TPU:0, one launch (start us, length us, event | category | flops | bytes accessed | tf_op | source)
XLA Modules:
  0.0 82.5 jit_solution(3917814926405038858)
XLA Ops:
  0.6 0.0 copy-start
  0.6 0.7 broadcast_subtract_fusion
  1.3 0.9 %fusion.2 = f32[2]{0:T(128)S(1)} fusion(bf16[2,4608]{1,0:T(2,128)(2,1)} %param.5), kind=kLoop, calls=%fused_computation.8 | loop fusion | flops 27646 | bytes 18440 | tf_op jit(solution)/shard_map/reduce_sum | solution.py:17
  2.2 0.8 %fusion.5 = bf16[1,2,4608]{2,1,0:T(2,128)(2,1)S(1)} fusion(f32[4608]{0:T(1024)} %param.6, f32[2]{0:T(128)S(1)} %add_rsqrt_fusion, bf16[2,4608]{1,0:T(2,128)(2,1)} %param.5), kind=kLoop, calls=%fused_computation.11 | loop fusion | flops 36864 | bytes 55304
  3.0 23.9 %all-gather = bf16[16,2,4608]{2,1,0:T(2,128)(2,1)S(1)} all-gather(bf16[1,2,4608]{2,1,0:T(2,128)(2,1)S(1)} %fusion.5), channel_id=1, replica_groups=mesh['tok'=2,'voc'=16] {'voc'}, dimensions={0}, use_global_device_ids=true | all-gather | bytes 313344 | tf_op jit(solution)/shard_map/all_gather | solution.py:21
  26.9 0.1 reshape.41
  27.1 9.9 %all_gather.7 = bf16[64,4608]{1,0:T(8,128)(2,1)S(1)} all-gather(bf16[32,4608]{1,0:T(8,128)(2,1)S(1)} %reshape.41), channel_id=1, replica_groups=mesh['tok'=2,'voc'=16] {'tok'}, dimensions={0}, use_global_device_ids=true | all-gather | bytes 884736 | tf_op jit(solution)/shard_map/all_gather | solution.py:23
  37.0 4.0 %exponential_reduce_fusion = (f32[64]{0:T(128)S(1)}, f32[64]{0:T(128)S(1)}) fusion(s32[64]{0:T(128)S(1)} %broadcast_subtract_fusion, bf16[64,4608]{1,0:T(8,128)(2,1)S(1)} %all_gather.7, bf16[512,4608]{1,0:T(8,128)(2,1)} %param.7), kind=kOutput, calls=%fused_computation.5 | convolution fusion | flops 302186368 | bytes 5309184 | tf_op jit(solution)/shard_map/dot_general | solution.py:22
  41.0 36.9 %psum.7 = f32[2,64]{1,0:T(2,128)S(1)} all-reduce(f32[2,64]{1,0:T(2,128)S(1)} %pad_maximum_fusion), channel_id=1, replica_groups=mesh['tok'=2,'voc'=16] {'tok','voc'}, use_global_device_ids=true, to_apply=%region_3.4 | all-reduce | flops 128 | bytes 1024 | tf_op jit(solution)/shard_map/psum | solution.py:37
  77.9 0.0 copy-done
  77.9 0.1 iota_compare_fusion.1
  77.9 0.1 lt.32
  78.0 0.6 dynamic_slice.3
  78.6 0.1 lt.34
  78.7 0.6 select_reduce_fusion.1
  79.3 0.7 convert_reduce_fusion
  (3 shorter events, 0.0 us)
Async XLA Ops:
  0.6 77.2 %copy-start = (s32[2]{0:T(128)S(1)}, s32[2]{0:T(128)}, u32[]{:S(2)}) copy-start(s32[2]{0:T(128)} %param.9) | copy-start | bytes 28
where the time goes:
time: 83.5 us; the launch traced here: 82.5 us
  blocking collectives  70.7 us (85%)
  matrix products  4 us (5%)
  other arithmetic  3.75 us (4%)
  between operations  3.17 us (4%)
  local copies, waits for them, and re-layouts  0.88 us (1%)
    psum x1, blocking collectives, body(): totals = lax.psum(stats, ('tok', 'voc'))  36.9 us
    all_gather x1, blocking collectives, body(): grouped = lax.all_gather(normed, 'voc', axis=0, tiled=True)  23.9 us
    all_gather x1, blocking collectives, body(): lax.all_gather(grouped, 'tok', axis=0, tiled=True)  9.92 us
    dot_general x1, matrix products, body(): lax.dot_general(lax.all_gather(grouped, 'tok', axis=0, tiled=True), head_...  4 us

commit v1 on v0

v1 whole, which is shorter than its diff:
```python
import functools

import jax
import jax.numpy as jnp
from jax import lax
from jax.experimental import pallas as pl
from jax.experimental.pallas import tpu as pltpu
from jax.sharding import PartitionSpec as P

WINDOW = 32
MESH = pl.DeviceIdType.MESH


def kernel(T, H, M, C, seqs, lengths, hidden_hbm, gain_hbm, targets_hbm, head_hbm, tok_out, mean_out,
           hid, gain, targets, head, slots, rows, stats,
           in_sem, head_sem, send_sem, recv_sem, stat_send, stat_recv):
    V = H * M * C
    N = T * V
    own, D = hid.shape
    vocab_rows = head.shape[0]
    pieces = head_sem.shape[0]
    piece = vocab_rows // pieces
    tokens = rows.shape[0]
    G = T * M
    fold = 8 // own
    t = lax.axis_index("tok")
    v = lax.axis_index("voc")
    h, m, c = v // (M * C), (v // C) % M, v % C
    g = t * M + m
    me = t * V + v

    def block(t_, h_, m_, c_):
        return t_ * V + (h_ * M + m_) * C + c_

    def where_a(k):
        return (t, (lax.rem(h + k, H) * M + m) * C + c)

    def where_b(j):
        g_ = lax.rem(g + j, G)
        return (g_ // M, (h * M + g_ % M) * C + c)

    def where_c(i):
        return (t, (h * M + m) * C + lax.rem(c + i, C))

    barrier = pltpu.get_barrier_semaphore()
    for count, where in ((H, where_a), (G, where_b), (C, where_c)):
        def greet(k, _, where=where):
            pl.semaphore_signal(barrier, inc=1, device_id=where(k), device_id_type=MESH)
            return 0
        lax.fori_loop(1, count, greet, 0)

    loads = [
        pltpu.make_async_copy(hidden_hbm, hid, in_sem.at[0]),
        pltpu.make_async_copy(gain_hbm, gain, in_sem.at[1]),
        pltpu.make_async_copy(targets_hbm, targets, in_sem.at[2]),
    ]
    for load in loads:
        load.start()
    heads = [
        pltpu.make_async_copy(head_hbm.at[pl.ds(p * piece, piece)], head.at[pl.ds(p * piece, piece)], head_sem.at[p])
        for p in range(pieces)
    ]
    for load in heads:
        load.start()
    loads[0].wait()
    loads[1].wait()
    values = hid[...].astype(jnp.float32)
    meansq = jnp.mean(values * values, axis=1, keepdims=True)
    normed = (values * lax.rsqrt(meansq + 1e-06) * gain[...]).astype(jnp.bfloat16)
    slots[me] = normed
    pl.semaphore_wait(barrier, (H - 1) + (G - 1) + (C - 1))

    def copy(b, number, device):
        return pltpu.make_async_remote_copy(
            src_ref=slots.at[b], dst_ref=slots.at[b], send_sem=send_sem.at[number], recv_sem=recv_sem.at[b],
            device_id=device, device_id_type=MESH)

    def arrived(b):
        copy(b, 0, where_a(1)).wait_recv()

    def merge(b):
        eight = pl.ds(pl.multiple_of(b // fold * 8, 8), 8)
        mine = lax.broadcasted_iota(jnp.int32, (8, 1), 0) // own == b % fold
        rows[eight, :] = jnp.where(mine, jnp.concatenate([slots[b].astype(jnp.float32)] * fold, axis=0), rows[eight, :])

    first_b = H - 1
    first_c = first_b + H * (G - 1)

    def send_a(k, _):
        copy(me, k - 1, where_a(k)).start()
        return 0

    def pass_b(k, b):
        def one(j, _):
            copy(b, first_b + k * (G - 1) + j - 1, where_b(j)).start()
            return 0
        lax.fori_loop(1, G, one, 0)

    def pass_c(n, b):
        def one(i, _):
            copy(b, first_c + n * (C - 1) + i - 1, where_c(i)).start()
            return 0
        lax.fori_loop(1, C, one, 0)

    lax.fori_loop(1, H, send_a, 0)
    pass_b(0, me)
    pass_c(0, me)
    merge(me)

    def take_a(k, _):
        b = block(t, lax.rem(h + k, H), m, c)
        arrived(b)
        pass_b(k, b)
        pass_c(k, b)
        merge(b)
        return 0
    lax.fori_loop(1, H, take_a, 0)

    def take_b(n, _):
        k, j = n // (G - 1), n % (G - 1) + 1
        g_ = lax.rem(g + j, G)
        b = block(g_ // M, lax.rem(h + k, H), g_ % M, c)
        arrived(b)
        pass_c(H + n, b)
        merge(b)
        return 0
    lax.fori_loop(0, H * (G - 1), take_b, 0)

    def take_c(n, _):
        i, r = n // (G * H) + 1, n % (G * H)
        k, g_ = r // G, lax.rem(g + r % G, G)
        b = block(g_ // M, lax.rem(h + k, H), g_ % M, lax.rem(c + i, C))
        arrived(b)
        merge(b)
        return 0
    lax.fori_loop(0, (C - 1) * G * H, take_c, 0)

    for load in heads:
        load.wait()
    logits = lax.dot_general(
        head[...], rows[...].astype(jnp.bfloat16), (((1,), (1,)), ((), ())), preferred_element_type=jnp.float32)
    capped = 30.0 * jnp.tanh(logits / 30.0)
    expsum = jnp.sum(jnp.exp(capped), axis=0, keepdims=True)
    loads[2].wait()
    wanted = targets[...] - me * vocab_rows
    column = lax.broadcasted_iota(jnp.int32, capped.shape, 0)
    picked = jnp.sum(jnp.where(column == wanted, capped, 0.0), axis=0, keepdims=True)
    stats[me] = jnp.concatenate([expsum, picked], axis=0)

    def stat_copy(b, k, device):
        return pltpu.make_async_remote_copy(
            src_ref=stats.at[b], dst_ref=stats.at[b], send_sem=stat_send.at[k], recv_sem=stat_recv.at[b],
            device_id=device, device_id_type=MESH)

    def stat_start(k, _):
        d = lax.rem(me + k, N)
        stat_copy(me, k - 1, (d // V, d % V)).start()
        return 0
    lax.fori_loop(1, N, stat_start, 0)

    def sent(k, _):
        copy(me, k, where_a(1)).wait_send()
        return 0
    lax.fori_loop(0, N - 1, sent, 0)

    lane = lax.broadcasted_iota(jnp.int32, (1, tokens), 1)
    live = jnp.zeros((1, tokens), jnp.float32)
    total = jnp.int32(0)
    for s in range(seqs):
        position = lane - s * WINDOW
        size = lengths[s]
        total = total + size
        live = live + jnp.where((position >= 0) & (position < size) & (position < WINDOW), 1.0, 0.0)

    def stat_take(k, _):
        stat_copy(lax.rem(me + k, N), k - 1, where_a(1)).wait_recv()
        return 0
    lax.fori_loop(1, N, stat_take, 0)
    def stat_sent(k, _):
        stat_copy(me, k - 1, where_a(1)).wait_send()
        return 0
    lax.fori_loop(1, N, stat_sent, 0)
    totals = jnp.sum(stats[...], axis=0)
    loss = live * (jnp.log(totals[0:1]) - totals[1:2])
    count = jnp.full((1, 1), total, jnp.int32).astype(jnp.float32)
    mean_out[...] = jnp.sum(loss, axis=1, keepdims=True) / count
    tok_out[...] = jnp.concatenate(
        [jnp.sum(jnp.where(lane == me * own + r, loss, 0.0), axis=1, keepdims=True) for r in range(own)], axis=1)


def solution(mesh):
    T, V = mesh.shape["tok"], mesh.shape["voc"]
    C = 2 if V % 2 == 0 else 1
    M = 2 if (V // C) % 2 == 0 else 1
    H = V // (C * M)
    N = T * V

    def body(hidden, norm_gain, head_weight, targets, lengths):
        own, D = hidden.shape
        vocab_rows = head_weight.shape[0]
        tokens = own * N
        pieces = 4 if vocab_rows % 64 == 0 else 1
        hbm = pl.BlockSpec(memory_space=pl.ANY)
        token_loss, mean_loss = pl.pallas_call(
            functools.partial(kernel, T, H, M, C, lengths.shape[0]),
            out_shape=(jax.ShapeDtypeStruct((1, own), jnp.float32), jax.ShapeDtypeStruct((1, 1), jnp.float32)),
            in_specs=[pl.BlockSpec(memory_space=pltpu.SMEM), hbm, hbm, hbm, hbm],
            out_specs=(pl.BlockSpec(memory_space=pltpu.VMEM), pl.BlockSpec(memory_space=pltpu.VMEM)),
            scratch_shapes=[
                pltpu.VMEM((own, D), jnp.bfloat16),
                pltpu.VMEM((1, D), jnp.float32),
                pltpu.VMEM((1, tokens), jnp.int32),
                pltpu.VMEM((vocab_rows, D), jnp.bfloat16),
                pltpu.VMEM((N, own, D), jnp.bfloat16),
                pltpu.VMEM((tokens, D), jnp.float32),
                pltpu.VMEM((N, 2, tokens), jnp.float32),
                pltpu.SemaphoreType.DMA((3,)),
                pltpu.SemaphoreType.DMA((pieces,)),
                pltpu.SemaphoreType.DMA((N - 1,)),
                pltpu.SemaphoreType.DMA((N,)),
                pltpu.SemaphoreType.DMA((N - 1,)),
                pltpu.SemaphoreType.DMA((N,)),
            ],
            compiler_params=pltpu.CompilerParams(
                collective_id=0, has_side_effects=True, vmem_limit_bytes=60 * 1024 * 1024),
        )(lengths, hidden, norm_gain.reshape(1, D), targets.reshape(1, tokens), head_weight)
        return token_loss.reshape(own), mean_loss.reshape(())

    in_specs = (P(("tok", "voc"), None), P(), P(("tok", "voc"), None), P(), P())
    out_specs = (P(("tok", "voc")), P())
    return jax.shard_map(body, mesh=mesh, in_specs=in_specs, out_specs=out_specs, check_vma=False)
```

time: 83.5 us -> 28.7 us (0.34)
  blocking collectives: 70.7 us -> 0 us
  Pallas kernels: 0 us -> 23.6 us
  matrix products: 4 us -> 0 us
  other arithmetic: 3.75 us -> 0 us
  local copies, waits for them, and re-layouts: 0.88 us -> 2.52 us
    psum x1 -> x0, blocking collectives: 36.9 us -> none  [body(): totals = lax.psum(stats, ('tok', 'voc'))]
    all_gather x2 -> x0, blocking collectives: 33.8 us -> none  [the longest x1 23.9 us: body(): grouped = lax.all_gather(normed, 'voc', axis=0, tiled=True)]
    pallas_call x0 -> x1, Pallas kernels: none -> 23.6 us  [body(): pl.pallas_call(functools.partial(kernel, T, H, M, C, lengths.shape[0]), o...]
    dot_general x1 -> x0, matrix products: 4 us -> none  [body(): lax.dot_general(lax.all_gather(grouped, 'tok', axis=0, tiled=True), head_...]
    reduce_sum x3 -> x0, other arithmetic: 2.16 us -> none  [the longest x1 0.87 us: body(): meansq = jnp.mean(values * values, axis=1, keepdims=True)]
    reshape x0 -> x1, local copies, waits for them, and re-layouts: none -> 1.34 us  [body(): norm_gain.reshape(1, D)]
    unnamed x3 -> x1, local copies, waits for them, and re-layouts: 0.12 us -> 1.18 us
where the time goes in v1:
time: 28.7 us; the launch traced here: 28.5 us
  Pallas kernels  23.6 us (82%)
  local copies, waits for them, and re-layouts  2.52 us (9%)
  between operations  2.38 us (8%)
    pallas_call x1, Pallas kernels, body(): pl.pallas_call(functools.partial(kernel, T, H, M, C, lengths.shape[0]), o...  23.6 us
    reshape x1, local copies, waits for them, and re-layouts, body(): norm_gain.reshape(1, D)  1.34 us
    unnamed x1, local copies, waits for them, and re-layouts  1.18 us

profile of v1, /device:TPU:0, one launch (start us, length us, event | category | flops | bytes accessed | tf_op | source)
XLA Modules:
  0.0 28.5 jit_solution(13929862073536713185)
XLA Ops:
  0.6 1.3 %reshape.16.gain_hbm = f32[1,4608]{1,0:T(1,128)} reshape(f32[4608]{0:T(1024)} %param.6) | data formatting | bytes 36864 | tf_op jit(solution)/shard_map/reshape | solution.py:226
  2.0 23.6 %shard_map.68 = (f32[1,2]{1,0:T(1,128)}, f32[1,1]{1,0:T(1,128)}) custom-call(s32[2]{0:T(128)} %lengths.1, bf16[2,4608]{1,0:T(2,128)(2,1)} %hidden_hbm.1, f32[1,4608]{1,0:T(1,128)} %reshape.16.gain_hbm, s32[1,64]{1,0:T(1,128)} %bitcast.3, bf16[512,4608]{1,0:T(8,128)(2,1)} %head_hbm.1), custom_call_target="tpu_custom_call" | custom-call | tf_op jit(solution)/shard_map/pallas_call | solution.py:204
  25.5 1.2 %copy.9 = f32[2]{0:T(128)} copy(f32[2]{0:T(128)} %bitcast.4) | data formatting | bytes 16

commit v2 on v1

v2 whole, which is shorter than its diff:
```python
import functools

import jax
import jax.numpy as jnp
from jax import lax
from jax.experimental import pallas as pl
from jax.experimental.pallas import tpu as pltpu
from jax.sharding import PartitionSpec as P

WINDOW = 32
MESH = pl.DeviceIdType.MESH


def loop(low, high, step):
    if high - low <= 32:
        for k in range(low, high):
            step(k, 0)
    else:
        lax.fori_loop(low, high, step, 0)


def kernel(T, H, M, C, seqs, lengths, hidden_hbm, gain_hbm, targets_hbm, head_hbm, tok_out, mean_out,
           hid, gain, targets, head, slots, stats,
           in_sem, head_sem, send_sem, recv_sem, stat_send, stat_recv):
    V = H * M * C
    N = T * V
    own, D = hid.shape
    vocab_rows = head.shape[0]
    pieces = head_sem.shape[0]
    piece = vocab_rows // pieces
    tokens = N * own
    G = T * M
    t = lax.axis_index("tok")
    v = lax.axis_index("voc")
    h, m, c = v // (M * C), (v // C) % M, v % C
    g = t * M + m
    me = t * V + v

    def block(t_, h_, m_, c_):
        return t_ * V + (h_ * M + m_) * C + c_

    def where_a(k):
        return (t, (lax.rem(h + k, H) * M + m) * C + c)

    def where_b(j):
        g_ = lax.rem(g + j, G)
        return (g_ // M, (h * M + g_ % M) * C + c)

    def where_c(i):
        return (t, (h * M + m) * C + lax.rem(c + i, C))

    barrier = pltpu.get_barrier_semaphore()
    for count, where in ((H, where_a), (G, where_b), (C, where_c)):
        def greet(k, _, where=where):
            pl.semaphore_signal(barrier, inc=1, device_id=where(k), device_id_type=MESH)
            return 0
        loop(1, count, greet)

    loads = [
        pltpu.make_async_copy(hidden_hbm, hid, in_sem.at[0]),
        pltpu.make_async_copy(gain_hbm, gain, in_sem.at[1]),
        pltpu.make_async_copy(targets_hbm, targets, in_sem.at[2]),
    ]
    for load in loads:
        load.start()
    heads = [
        pltpu.make_async_copy(head_hbm.at[pl.ds(p * piece, piece)], head.at[pl.ds(p * piece, piece)], head_sem.at[p])
        for p in range(pieces)
    ]
    for load in heads:
        load.start()
    loads[0].wait()
    loads[1].wait()
    values = hid[...].astype(jnp.float32)
    meansq = jnp.mean(values * values, axis=1, keepdims=True)
    normed = (values * lax.rsqrt(meansq + 1e-06) * gain[...].reshape(1, D)).astype(jnp.bfloat16)
    slots[me] = normed
    pl.semaphore_wait(barrier, (H - 1) + (G - 1) + (C - 1))

    def copy(b, sem, device):
        return pltpu.make_async_remote_copy(
            src_ref=slots.at[b], dst_ref=slots.at[b], send_sem=send_sem.at[0], recv_sem=recv_sem.at[sem],
            device_id=device, device_id_type=MESH)

    def blocks(first, number, sem):
        part = slots.at[pl.ds(first, number)]
        return pltpu.make_async_remote_copy(
            src_ref=part, dst_ref=part, send_sem=send_sem.at[0], recv_sem=recv_sem.at[sem],
            device_id=where_a(1), device_id_type=MESH)

    def arrived(b):
        copy(b, b, where_a(1)).wait_recv()

    def send_a(k, _):
        copy(me, me, where_a(k)).start()
        return 0

    def pass_b(b):
        def one(j, _):
            copy(b, b, where_b(j)).start()
            return 0
        loop(1, G, one)

    def pass_c(b):
        def one(i, _):
            copy(b, N, where_c(i)).start()
            return 0
        loop(1, C, one)

    loop(1, H, send_a)
    pass_b(me)
    pass_c(me)

    def take_a(k, _):
        b = block(t, lax.rem(h + k, H), m, c)
        arrived(b)
        pass_b(b)
        pass_c(b)
        return 0
    loop(1, H, take_a)

    def take_b(n, _):
        k, j = n // (G - 1), n % (G - 1) + 1
        g_ = lax.rem(g + j, G)
        b = block(g_ // M, lax.rem(h + k, H), g_ % M, c)
        arrived(b)
        pass_c(b)
        return 0
    loop(0, H * (G - 1), take_b)

    if C > 1:
        blocks(0, (C - 1) * G * H, N).wait_recv()

    for load in heads:
        load.wait()
    logits = lax.dot_general(
        head[...], slots[...].reshape(tokens, D), (((1,), (1,)), ((), ())), preferred_element_type=jnp.float32)
    capped = 30.0 * jnp.tanh(logits / 30.0)
    expsum = jnp.sum(jnp.exp(capped), axis=0, keepdims=True)
    loads[2].wait()
    wanted = targets[...] - me * vocab_rows
    column = lax.broadcasted_iota(jnp.int32, capped.shape, 0)
    picked = jnp.sum(jnp.where(column == wanted, capped, 0.0), axis=0, keepdims=True)
    stats[me] = jnp.concatenate([expsum, picked], axis=0)

    def stat_copy(b, k, device):
        return pltpu.make_async_remote_copy(
            src_ref=stats.at[b], dst_ref=stats.at[b], send_sem=stat_send.at[0], recv_sem=stat_recv.at[0],
            device_id=device, device_id_type=MESH)

    def stat_start(k, _):
        d = lax.rem(me + k, N)
        stat_copy(me, k - 1, (d // V, d % V)).start()
        return 0
    loop(1, N, stat_start)

    blocks(0, N - 1, 0).wait_send()

    lane = lax.broadcasted_iota(jnp.int32, (1, tokens), 1)
    live = jnp.zeros((1, tokens), jnp.float32)
    total = jnp.int32(0)
    for s in range(seqs):
        position = lane - s * WINDOW
        size = lengths[s]
        total = total + size
        live = live + jnp.where((position >= 0) & (position < size) & (position < WINDOW), 1.0, 0.0)

    everyone = pltpu.make_async_remote_copy(
        src_ref=stats.at[pl.ds(0, N - 1)], dst_ref=stats.at[pl.ds(0, N - 1)], send_sem=stat_send.at[0],
        recv_sem=stat_recv.at[0], device_id=where_a(1), device_id_type=MESH)
    everyone.wait_send()
    everyone.wait_recv()
    totals = jnp.sum(stats[...], axis=0)
    loss = live * (jnp.log(totals[0:1]) - totals[1:2])
    mean_out[0] = jnp.sum(loss) / total.astype(jnp.float32)
    for r in range(own):
        tok_out[r] = jnp.sum(jnp.where(lane == me * own + r, loss, 0.0))


def solution(mesh):
    T, V = mesh.shape["tok"], mesh.shape["voc"]
    C = 2 if V % 2 == 0 else 1
    M = 2 if (V // C) % 2 == 0 else 1
    H = V // (C * M)
    N = T * V

    def body(hidden, norm_gain, head_weight, targets, lengths):
        own, D = hidden.shape
        vocab_rows = head_weight.shape[0]
        tokens = own * N
        pieces = 4 if vocab_rows % 64 == 0 else 1
        hbm = pl.BlockSpec(memory_space=pl.ANY)
        token_loss, mean_loss = pl.pallas_call(
            functools.partial(kernel, T, H, M, C, lengths.shape[0]),
            out_shape=(jax.ShapeDtypeStruct((own,), jnp.float32), jax.ShapeDtypeStruct((1,), jnp.float32)),
            in_specs=[pl.BlockSpec(memory_space=pltpu.SMEM), hbm, hbm, hbm, hbm],
            out_specs=(pl.BlockSpec(memory_space=pltpu.SMEM), pl.BlockSpec(memory_space=pltpu.SMEM)),
            scratch_shapes=[
                pltpu.VMEM((own, D), jnp.bfloat16),
                pltpu.VMEM((D,), jnp.float32),
                pltpu.VMEM((1, tokens), jnp.int32),
                pltpu.VMEM((vocab_rows, D), jnp.bfloat16),
                pltpu.VMEM((N, own, D), jnp.bfloat16),
                pltpu.VMEM((N, 2, tokens), jnp.float32),
                pltpu.SemaphoreType.DMA((3,)),
                pltpu.SemaphoreType.DMA((pieces,)),
                pltpu.SemaphoreType.DMA((1,)),
                pltpu.SemaphoreType.DMA((N + 1,)),
                pltpu.SemaphoreType.DMA((1,)),
                pltpu.SemaphoreType.DMA((1,)),
            ],
            compiler_params=pltpu.CompilerParams(
                collective_id=0, has_side_effects=True, vmem_limit_bytes=60 * 1024 * 1024),
        )(lengths, hidden, norm_gain, targets.reshape(1, tokens), head_weight)
        return token_loss, mean_loss.reshape(())

    in_specs = (P(("tok", "voc"), None), P(), P(("tok", "voc"), None), P(), P())
    out_specs = (P(("tok", "voc")), P())
    return jax.shard_map(body, mesh=mesh, in_specs=in_specs, out_specs=out_specs, check_vma=False)
```

time: 28.7 us -> 25.3 us (0.88)
  Pallas kernels: 23.6 us -> 21.7 us
  local copies, waits for them, and re-layouts: 2.52 us -> 1.11 us
    pallas_call x1, Pallas kernels: 23.6 us -> 21.7 us  [body(): pl.pallas_call(functools.partial(kernel, T, H, M, C, lengths.shape[0]), o...]
    reshape x1 -> x0, local copies, waits for them, and re-layouts: 1.34 us -> none  [body(): norm_gain.reshape(1, D)]
where the time goes in v2:
time: 25.3 us; the launch traced here: 25.2 us
  Pallas kernels  21.7 us (86%)
  between operations  2.4 us (9%)
  local copies, waits for them, and re-layouts  1.11 us (4%)
    pallas_call x1, Pallas kernels, body(): pl.pallas_call(functools.partial(kernel, T, H, M, C, lengths.shape[0]), o...  21.7 us
    unnamed x1, local copies, waits for them, and re-layouts  1.11 us

profile of v2, /device:TPU:0, one launch (start us, length us, event | category | flops | bytes accessed | tf_op | source)
XLA Modules:
  0.0 25.2 jit_solution(16808066326740698433)
XLA Ops:
  0.6 21.7 %shard_map.68 = (f32[2]{0:T(128)}, f32[1]{0:T(128)}) custom-call(s32[2]{0:T(128)} %lengths.1, bf16[2,4608]{1,0:T(2,128)(2,1)} %hidden_hbm.1, f32[4608]{0:T(1024)} %gain_hbm.1, s32[1,64]{1,0:T(1,128)} %bitcast.2, bf16[512,4608]{1,0:T(8,128)(2,1)} %head_hbm.1), custom_call_target="tpu_custom_call" | custom-call | tf_op jit(solution)/shard_map/pallas_call | solution.py:193
  22.3 1.1 %copy.9 = f32[2]{0:T(128)} copy(f32[2]{0:T(128)} %get-tuple-element.8) | data formatting | bytes 16

commit v3 on v2

--- a/solution.py
+++ b/solution.py
@@ -17,6 +17,12 @@
             step(k, 0)
     else:
         lax.fori_loop(low, high, step, 0)
+
+
+def other(mine, k, size):
+    if size & (size - 1) == 0:
+        return mine ^ k
+    return lax.rem(mine + k, size)
 
 
 def kernel(T, H, M, C, seqs, lengths, hidden_hbm, gain_hbm, targets_hbm, head_hbm, tok_out, mean_out,
@@ -40,21 +46,14 @@
         return t_ * V + (h_ * M + m_) * C + c_
 
     def where_a(k):
-        return (t, (lax.rem(h + k, H) * M + m) * C + c)
+        return (t, (other(h, k, H) * M + m) * C + c)
 
     def where_b(j):
-        g_ = lax.rem(g + j, G)
+        g_ = other(g, j, G)
         return (g_ // M, (h * M + g_ % M) * C + c)
 
     def where_c(i):
-        return (t, (h * M + m) * C + lax.rem(c + i, C))
-
-    barrier = pltpu.get_barrier_semaphore()
-    for count, where in ((H, where_a), (G, where_b), (C, where_c)):
-        def greet(k, _, where=where):
-            pl.semaphore_signal(barrier, inc=1, device_id=where(k), device_id_type=MESH)
-            return 0
-        loop(1, count, greet)
+        return (t, (h * M + m) * C + other(c, i, C))
 
     loads = [
         pltpu.make_async_copy(hidden_hbm, hid, in_sem.at[0]),
@@ -63,12 +62,13 @@
     ]
     for load in loads:
         load.start()
-    heads = [
-        pltpu.make_async_copy(head_hbm.at[pl.ds(p * piece, piece)], head.at[pl.ds(p * piece, piece)], head_sem.at[p])
-        for p in range(pieces)
-    ]
-    for load in heads:
-        load.start()
+    barrier = pltpu.get_barrier_semaphore()
+    for count, where in ((H, where_a), (G, where_b), (C, where_c)):
+        def greet(k, _, where=where):
+            pl.semaphore_signal(barrier, inc=1, device_id=where(k), device_id_type=MESH)
+            return 0
+        loop(1, count, greet)
+
     loads[0].wait()
     loads[1].wait()
     values = hid[...].astype(jnp.float32)
@@ -92,12 +92,12 @@
         copy(b, b, where_a(1)).wait_recv()
 
     def send_a(k, _):
-        copy(me, me, where_a(k)).start()
+        copy(me, me, where_a(H - k)).start()
         return 0
 
     def pass_b(b):
         def one(j, _):
-            copy(b, b, where_b(j)).start()
+            copy(b, b, where_b(G - j)).start()
             return 0
         loop(1, G, one)
 
@@ -111,8 +111,15 @@
     pass_b(me)
     pass_c(me)
 
+    heads = [
+        pltpu.make_async_copy(head_hbm.at[pl.ds(p * piece, piece)], head.at[pl.ds(p * piece, piece)], head_sem.at[p])
+        for p in range(pieces)
+    ]
+    for load in heads:
+        load.start()
+
     def take_a(k, _):
-        b = block(t, lax.rem(h + k, H), m, c)
+        b = block(t, other(h, k, H), m, c)
         arrived(b)
         pass_b(b)
         pass_c(b)
@@ -121,8 +128,8 @@
 
     def take_b(n, _):
         k, j = n // (G - 1), n % (G - 1) + 1
-        g_ = lax.rem(g + j, G)
-        b = block(g_ // M, lax.rem(h + k, H), g_ % M, c)
+        g_ = other(g, j, G)
+        b = block(g_ // M, other(h, k, H), g_ % M, c)
         arrived(b)
         pass_c(b)
         return 0
@@ -149,7 +156,7 @@
             device_id=device, device_id_type=MESH)
 
     def stat_start(k, _):
-        d = lax.rem(me + k, N)
+        d = other(me, N - k, N)
         stat_copy(me, k - 1, (d // V, d % V)).start()
         return 0
     loop(1, N, stat_start)

time: 25.3 us -> 24.3 us (0.960)
  Pallas kernels: 21.7 us -> 20.6 us
    pallas_call x1, Pallas kernels: 21.7 us -> 20.6 us  [body(): pl.pallas_call(functools.partial(kernel, T, H, M, C, lengths.shape[0]), o...]
where the time goes in v3:
time: 24.3 us; the launch traced here: 24.1 us
  Pallas kernels  20.6 us (85%)
  between operations  2.4 us (10%)
  local copies, waits for them, and re-layouts  1.11 us (5%)
    pallas_call x1, Pallas kernels, body(): pl.pallas_call(functools.partial(kernel, T, H, M, C, lengths.shape[0]), o...  20.6 us
    unnamed x1, local copies, waits for them, and re-layouts  1.11 us

profile of v3, /device:TPU:0, one launch (start us, length us, event | category | flops | bytes accessed | tf_op | source)
XLA Modules:
  0.0 24.1 jit_solution(8786088684199468833)
XLA Ops:
  0.6 20.6 %shard_map.68 = (f32[2]{0:T(128)}, f32[1]{0:T(128)}) custom-call(s32[2]{0:T(128)} %lengths.1, bf16[2,4608]{1,0:T(2,128)(2,1)} %hidden_hbm.1, f32[4608]{0:T(1024)} %gain_hbm.1, s32[1,64]{1,0:T(1,128)} %bitcast.2, bf16[512,4608]{1,0:T(8,128)(2,1)} %head_hbm.1), custom_call_target="tpu_custom_call" | custom-call | tf_op jit(solution)/shard_map/pallas_call | solution.py:200
  21.2 1.1 %copy.9 = f32[2]{0:T(128)} copy(f32[2]{0:T(128)} %get-tuple-element.8) | data formatting | bytes 16

commit v4 on v3

--- a/solution.py
+++ b/solution.py
@@ -148,7 +148,7 @@
     wanted = targets[...] - me * vocab_rows
     column = lax.broadcasted_iota(jnp.int32, capped.shape, 0)
     picked = jnp.sum(jnp.where(column == wanted, capped, 0.0), axis=0, keepdims=True)
-    stats[me] = jnp.concatenate([expsum, picked], axis=0)
+    stats[me] = jnp.concatenate([expsum, picked], axis=1)
 
     def stat_copy(b, k, device):
         return pltpu.make_async_remote_copy(
@@ -178,7 +178,7 @@
     everyone.wait_send()
     everyone.wait_recv()
     totals = jnp.sum(stats[...], axis=0)
-    loss = live * (jnp.log(totals[0:1]) - totals[1:2])
+    loss = live * (jnp.log(totals[:, :tokens]) - totals[:, tokens:])
     mean_out[0] = jnp.sum(loss) / total.astype(jnp.float32)
     for r in range(own):
         tok_out[r] = jnp.sum(jnp.where(lane == me * own + r, loss, 0.0))
@@ -208,7 +208,7 @@
                 pltpu.VMEM((1, tokens), jnp.int32),
                 pltpu.VMEM((vocab_rows, D), jnp.bfloat16),
                 pltpu.VMEM((N, own, D), jnp.bfloat16),
-                pltpu.VMEM((N, 2, tokens), jnp.float32),
+                pltpu.VMEM((N, 1, 2 * tokens), jnp.float32),
                 pltpu.SemaphoreType.DMA((3,)),
                 pltpu.SemaphoreType.DMA((pieces,)),
                 pltpu.SemaphoreType.DMA((1,)),

time: 24.3 us -> 24.3 us (level)
  no operation moved by 1% of the time
where the time goes in v4:
time: 24.3 us; the launch traced here: 24.1 us
  Pallas kernels  20.6 us (85%)
  between operations  2.4 us (10%)
  local copies, waits for them, and re-layouts  1.11 us (5%)
    pallas_call x1, Pallas kernels, body(): pl.pallas_call(functools.partial(kernel, T, H, M, C, lengths.shape[0]), o...  20.6 us
    unnamed x1, local copies, waits for them, and re-layouts  1.11 us

profile of v4, /device:TPU:0, one launch (start us, length us, event | category | flops | bytes accessed | tf_op | source)
XLA Modules:
  0.0 24.1 jit_solution(17897312874242796263)
XLA Ops:
  0.6 20.6 %shard_map.68 = (f32[2]{0:T(128)}, f32[1]{0:T(128)}) custom-call(s32[2]{0:T(128)} %lengths.1, bf16[2,4608]{1,0:T(2,128)(2,1)} %hidden_hbm.1, f32[4608]{0:T(1024)} %gain_hbm.1, s32[1,64]{1,0:T(1,128)} %bitcast.2, bf16[512,4608]{1,0:T(8,128)(2,1)} %head_hbm.1), custom_call_target="tpu_custom_call" | custom-call | tf_op jit(solution)/shard_map/pallas_call | solution.py:200
  21.2 1.1 %copy.9 = f32[2]{0:T(128)} copy(f32[2]{0:T(128)} %get-tuple-element.8) | data formatting | bytes 16
